TPU v7x, 32 devices: a whole 2x2x4 slice. The times are simulated.
32 devices in a mesh: groups: 2 (over y), gy: 4 (over z), gz: 4 (over x, core).
Axes of the slice: x: 2, y: 2, z: 4, core: 2. Of those that a mesh axis runs over, the one named last changes fastest.
Arguments:
- indirect: float32 [4, 512, 32, 512], P('groups', 'gy', 'gz'), parts along dimension 0, may hold values from -6 to 6
- past_indirect: float32 [8, 2, 512, 32, 512], P('groups', None, 'gy', 'gz'), parts along dimension 0, may hold values from -6 to 6
- past_residual: float32 [8, 2, 512, 32, 512], P('groups', None, 'gy', 'gz'), parts along dimension 0, may hold values from -40 to 40
- atom_table: float32 [10, 4, 4, 128], P('groups', 'gy', 'gz'), parts along dimension 0, may hold values from -4 to 512, as said below
- atom_counts: int32 [8, 4], P(('groups', 'gy'), 'gz'), parts along dimension 0, may hold values from 1 to 128, as said below
- chi_amps: float32 [3, 4], replicated, may hold values from -3 to 3
- chi_widths: float32 [4], replicated, may hold values from 0.5 to 4
Outputs:
- new_indirect: float32 [4, 512, 32, 512], P('groups', 'gy', 'gz'), parts along dimension 0
- residual: float32 [4, 512, 32, 512], P('groups', 'gy', 'gz'), parts along dimension 0
There are 2 independent parts, one for each index of `groups`. A program takes and returns all parts, laid end to end along the dimension named above; an argument that names none is the same for every part. Nothing has to cross between parts.
Inputs may be any that keep to these rules, and one draw needn't show every extreme that they name: `atom_counts`: some pencil has exactly 128 live rows in every draw. `atom_table`: each row of pencil (p, q) has its y position in [p * 128, (p + 1) * 128) and its z position in [q * 8, (q + 1) * 8); x positions lie in [0, 512).
All inputs are finite; a program needn't handle non-finite values.
Results may differ from a plain program's by a relative error of at most 0.0003.
Values sent between devices are 32-bit elements; how exact they have to be, the bound alone decides.
A program may use at most 192 MiB of HBM per device.

v0:
```python
import math
import jax
import jax.numpy as jnp
from jax import lax
from jax.sharding import PartitionSpec as P

SIGX = 8
PRECISE = lax.Precision.HIGHEST
MIX_STEP = 0.3
BOND_OH = 1.9
BOND_HH = 3.1


def with_halo(cells, sides, width):
    for axis, dim in sides:
        count = lax.axis_size(axis)
        head = lax.slice_in_dim(cells, 0, width, axis=dim)
        tail = lax.slice_in_dim(cells, cells.shape[dim] - width, cells.shape[dim], axis=dim)
        cells = jnp.concatenate(
            [
                lax.ppermute(tail, axis, [(i, (i + 1) % count) for i in range(count)]),
                cells,
                lax.ppermute(head, axis, [((i + 1) % count, i) for i in range(count)]),
            ],
            axis=dim,
        )
    return cells


def hartley(length):
    position = lax.iota(jnp.int32, length)
    product = position[:, None] * position[None, :] % length
    angle = product.astype(jnp.float32) * (2.0 * math.pi / length)
    return (jnp.cos(angle) + jnp.sin(angle)) / math.sqrt(length)


def wave_squared(position, length):
    folded = jnp.where(2 * position > length, position - length, position)
    scaled = folded.astype(jnp.float32) * (2.0 * math.pi / length)
    return scaled * scaled


def response(wave_square, chi_amps, chi_widths):
    wavenumber = jnp.sqrt(wave_square)
    summed = [jnp.zeros_like(wave_square) for channel in range(3)]
    for which_term in range(chi_widths.shape[0]):
        gaussian_term = jnp.exp(-wave_square * (chi_widths[which_term] * chi_widths[which_term]))
        summed = [
            summed[channel] + chi_amps[channel, which_term] * gaussian_term for channel in range(3)
        ]
    oxygen = 1.0 + summed[0]
    mixed_site = 2.0 * jnp.sinc(wavenumber * (BOND_OH / math.pi)) + summed[1]
    hydrogen = 2.0 + 2.0 * jnp.sinc(wavenumber * (BOND_HH / math.pi)) + summed[2]
    return (oxygen, mixed_site, hydrogen)


def couple(spectrum, wave_square, chi_amps, chi_widths):
    oxygen, mixed_site, hydrogen = response(wave_square, chi_amps, chi_widths)
    return jnp.stack(
        [
            oxygen * spectrum[0] + mixed_site * spectrum[1],
            mixed_site * spectrum[0] + hydrogen * spectrum[1],
        ]
    )


def gaussian(offset, length, spread):
    offset = offset - length * jnp.floor(offset / length + 0.5)
    return jnp.exp(-0.5 * offset * offset / (spread * spread))


def pencil_field(
    atom_rows, pencil_y, pencil_z, cells_y, cells_z, total_x, total_y, total_z, spread_x
):
    cell_y = (pencil_y * cells_y + lax.iota(jnp.int32, cells_y)).astype(jnp.float32)
    cell_z = (pencil_z * cells_z + lax.iota(jnp.int32, cells_z)).astype(jnp.float32)
    cell_x = lax.iota(jnp.int32, total_x).astype(jnp.float32)
    along_y = gaussian(cell_y[:, None] - atom_rows[1][None, :], total_y, 0.5 * cells_y)
    along_z = gaussian(cell_z[:, None] - atom_rows[2][None, :], total_z, 0.5 * cells_z)
    along_x = gaussian(cell_x[:, None] - atom_rows[0][None, :], total_x, spread_x)
    left = atom_rows[3:5][:, None, None, :] * along_y[None, :, None, :] * along_z[None, None, :, :]
    left = left.reshape(2, cells_y * cells_z, atom_rows.shape[1])
    return jnp.einsum("sra,xa->srx", left, along_x, precision=PRECISE)


def body(indirect, past_indirect, past_residual, atom_table, atom_counts, chi_amps, chi_widths):
    cells_y = indirect.shape[1]
    cells_z = indirect.shape[2]
    cells_x = indirect.shape[3]
    parts_y = lax.axis_size("gy")
    parts_z = lax.axis_size("gz")
    total_y = cells_y * parts_y
    total_z = cells_z * parts_z
    row_count = atom_table.shape[3]
    present = (lax.iota(jnp.int32, row_count) < atom_counts[0, 0]).astype(jnp.float32)
    bucket = jnp.concatenate([atom_table[0:3], atom_table[3:5] * present], 0)
    nearby = with_halo(bucket, (("gy", 1), ("gz", 2)), 1)
    nearby = nearby.reshape(5, 9 * row_count)
    potential_field = pencil_field(
        nearby,
        lax.axis_index("gy"),
        lax.axis_index("gz"),
        cells_y,
        cells_z,
        cells_x,
        total_y,
        total_z,
        float(SIGX),
    )
    potential_field = potential_field.reshape(2, cells_y, cells_z, cells_x)
    argument = indirect - potential_field
    closed = jnp.where(argument > 0, argument, jnp.expm1(jnp.minimum(argument, 0.0)))
    direct = closed - indirect
    table_x = hartley(cells_x)
    table_y = hartley(total_y)
    table_z = hartley(total_z)
    blocks = parts_y * parts_z
    width_x = cells_x // blocks
    grid_y = table_y.reshape(parts_y, cells_y, total_y)
    grid_z = table_z.reshape(parts_z, cells_z, total_z)
    outgoing = jnp.einsum(
        "scdx,xqk->sqkdc", direct, table_x.reshape(cells_x, blocks, width_x), precision=PRECISE
    )
    outgoing = outgoing.reshape(2, blocks, 1, width_x * cells_z * cells_y)
    received = lax.all_to_all(outgoing, ("gy", "gz"), split_axis=1, concat_axis=2, tiled=True)
    count = received.shape[0]
    pieces = received.reshape(count, parts_y, parts_z, width_x, cells_z, cells_y)
    partial_value = jnp.einsum("sabxdc,acy->sbxdy", pieces, grid_y, precision=PRECISE)
    section_two = jnp.einsum("sbxdy,bdz->sxzy", partial_value, grid_z, precision=PRECISE)
    wave_x = wave_squared(
        lax.axis_index(("gy", "gz")) * width_x + lax.iota(jnp.int32, width_x), cells_x
    )
    wave_square = (
        wave_x[:, None, None]
        + wave_squared(lax.iota(jnp.int32, total_z), total_z)[None, :, None]
        + wave_squared(lax.iota(jnp.int32, total_y), total_y)[None, None, :]
    )
    coupled = couple(section_two, wave_square, chi_amps, chi_widths)
    partial_value = jnp.einsum("sxzy,bdz->sxbdy", coupled, grid_z, precision=PRECISE)
    returning = jnp.einsum("sxbdy,acy->sabxdc", partial_value, grid_y, precision=PRECISE)
    returning = returning.reshape(2, blocks, 1, width_x * cells_z * cells_y)
    table_back = table_x.reshape(blocks, width_x, cells_x)
    received = lax.all_to_all(returning, ("gy", "gz"), split_axis=1, concat_axis=2, tiled=True)
    count = received.shape[0]
    pieces = received.reshape(count, blocks, width_x, cells_z, cells_y)
    summed_field = jnp.einsum("sqxdc,qxk->scdk", pieces, table_back, precision=PRECISE)
    residual = summed_field - direct - indirect
    stacked = jnp.concatenate([residual[None], past_residual], 0)
    gram_matrix = jnp.einsum("isyzx,jsyzx->ij", stacked, stacked, precision=PRECISE)
    gram_matrix = lax.psum(gram_matrix, ("gy", "gz"))
    factor = jnp.linalg.cholesky(gram_matrix)
    weights = jax.scipy.linalg.cho_solve(
        (factor, True), jnp.ones((gram_matrix.shape[0],), jnp.float32)
    )
    mixing = weights / jnp.sum(weights)
    earlier = jnp.einsum(
        "i,isyzx->syzx", mixing[1:], past_indirect + MIX_STEP * past_residual, precision=PRECISE
    )
    new_indirect = mixing[0] * (indirect + MIX_STEP * residual) + earlier
    return (new_indirect, residual)


def solution(mesh):
    return jax.shard_map(
        body,
        mesh=mesh,
        in_specs=(
            P("groups", "gy", "gz", None),
            P("groups", None, "gy", "gz", None),
            P("groups", None, "gy", "gz", None),
            P("groups", "gy", "gz", None),
            P(("groups", "gy"), "gz"),
            P(),
            P(),
        ),
        out_specs=(P("groups", "gy", "gz", None), P("groups", "gy", "gz", None)),
        check_vma=False,
    )
```

profile of v0, /device:TPU:0, one launch (start us, length us, event | category | flops | bytes accessed | tf_op | source)
XLA Modules:
  0.0 549.4 jit_solution(14519221556603764568)
XLA Ops:
  13.1 18.8 %fusion.6 = f32[2,128,8,512]{3,1,2,0:T(8,128)S(1)} fusion(f32[8,1152]{1,0:T(8,128)S(1)} %fusion.224, f32[2,128,1152]{2,1,0:T(8,128)S(1)} %broadcast_multiply_fusion, f32[1152]{0:T(1024)S(1)} %sub.111, f32[512]{0:T(512)S(1)} %iota_convert_fusion), kind=kOutput, calls=%fused_computation.8 | convolution fusion | flops 14503182336 | bytes 5417472 | tf_op jit(solution)/shard_map/sra,xa->srx/dot_general | solution.py:83
  31.9 14.1 %fusion.56 = f32[2,16,32,8,128]{4,2,3,0,1:T(8,128)S(1)} fusion(f32[2,128,8,512]{3,1,2,0:T(8,128)S(1)} %fusion.6, f32[2,128,8,512]{3,2,1,0:T(8,128)S(1)} %copy-done.2, s32[16,32]{1,0:T(8,128)S(1)} %multiply_add_fusion.3), kind=kOutput, calls=%fused_computation.68 | convolution fusion | flops 6451888128 | bytes 12584960 | tf_op jit(solution)/shard_map/scdx,xqk->sqkdc/dot_general | solution.py:121
  46.0 5.8 %copy.90 = f32[2,16,32,8,128]{4,3,2,0,1:T(8,128)} copy(f32[2,16,32,8,128]{4,2,3,0,1:T(8,128)S(1)} %fusion.56) | data formatting | bytes 8388608 | tf_op jit(solution)/shard_map/reshape | solution.py:124
  51.8 5.9 %reshape.439 = f32[2,16,1,32768]{3,0,2,1:T(2,128)} reshape(f32[2,16,32,8,128]{4,3,2,0,1:T(8,128)} %copy.90) | data formatting | bytes 8388608 | tf_op jit(solution)/shard_map/reshape | solution.py:124
  57.8 6.7 %all-to-all-start = ((f32[2,16,1,32768]{3,0,2,1:T(2,128)}), f32[2,16,1,32768]{3,0,2,1:T(2,128)}, u32[]{:S(2)}, u32[]{:S(2)}) async-start(f32[2,16,1,32768]{3,0,2,1:T(2,128)} %reshape.439), calls=%async_computation | async-start | bytes 8388608 | tf_op jit(solution)/shard_map/all_to_all | solution.py:125
  71.0 71.0 %all-to-all-done = f32[2,16,1,32768]{3,0,2,1:T(2,128)} async-done(((f32[2,16,1,32768]{3,0,2,1:T(2,128)}), f32[2,16,1,32768]{3,0,2,1:T(2,128)}, u32[]{:S(2)}, u32[]{:S(2)}) %all-to-all-start) | async-done | bytes 4194336 | tf_op jit(solution)/shard_map/all_to_all | solution.py:125
  142.1 7.0 %reshape.440 = f32[2,4,4,32,8,128]{5,4,3,0,2,1:T(8,128)} reshape(f32[2,16,1,32768]{3,0,2,1:T(2,128)} %all-to-all-done) | data formatting | bytes 8388608 | tf_op jit(solution)/shard_map/reshape | solution.py:127
  149.1 13.7 %fusion.21 = f32[2,4,32,8,512,1]{4,3,5,1,2,0:T(8,128)S(1)} fusion(f32[2,4,4,32,8,128]{5,4,3,0,2,1:T(8,128)} %reshape.440, s32[4,128]{1,0:T(4,128)S(1)} %multiply_add_fusion.5), kind=kOutput, calls=%fused_computation.26 | convolution fusion | flops 6446645248 | bytes 8390656 | tf_op jit(solution)/shard_map/sabxdc,acy->sbxdy/dot_general | solution.py:128
  167.2 12.9 %fusion.101 = f32[1,32,32,512]{3,2,1,0:T(8,128)S(1)} fusion(f32[2,32,32,512]{3,2,1,0:T(8,128)S(1)} %fusion.59, f32[]{:T(128)} %bitcast.42, f32[]{:T(128)} %bitcast.41, f32[]{:T(128)} %bitcast.40, f32[]{:T(128)} %bitcast.39, f32[]{:T(128)} %bitcast.14, f32[]{:T(128)} %bitcast.12, f32[]{:T(128)} %bitcast.10, f32[]{:T(128)} %bitcast.8, f32[512]{0:T(512)S(1)} %fusion.240, ...), kind=kLoop, calls=%fused_computation.107 | loop fusion | flops 50331648 | bytes 6297648 | tf_op jit(solution)/shard_map/stack | solution.py:59
  180.0 10.3 %fusion.90 = f32[1,32,32,512]{3,2,1,0:T(8,128)S(1)} fusion(f32[2,32,32,512]{3,2,1,0:T(8,128)S(1)} %fusion.59, f32[]{:T(128)} %bitcast.14, f32[]{:T(128)} %bitcast.13, f32[]{:T(128)} %bitcast.12, f32[]{:T(128)} %bitcast.11, f32[]{:T(128)} %bitcast.10, f32[]{:T(128)} %bitcast.9, f32[]{:T(128)} %bitcast.8, f32[512]{0:T(512)S(1)} %fusion.240, ...), kind=kLoop, calls=%fused_computation.96 | loop fusion | flops 31457280 | bytes 6297648 | tf_op jit(solution)/shard_map/stack | solution.py:59
  194.5 13.6 %fusion.63 = f32[2,4,4,32,8,128]{5,3,4,2,0,1:T(8,128)S(1)} fusion(f32[2,32,4,8,512]{4,3,1,0,2:T(8,128)S(1)} %fusion.62, s32[4,128]{1,0:T(4,128)S(1)} %multiply_add_fusion.5), kind=kOutput, calls=%fused_computation.71 | convolution fusion | flops 6446645248 | bytes 8390656 | tf_op jit(solution)/shard_map/sxbdy,acy->sabxdc/dot_general | solution.py:140
  208.0 5.8 %copy.93 = f32[2,4,4,32,8,128]{5,4,3,0,2,1:T(8,128)} copy(f32[2,4,4,32,8,128]{5,3,4,2,0,1:T(8,128)S(1)} %fusion.63) | data formatting | bytes 8388608 | tf_op jit(solution)/shard_map/reshape | solution.py:141
  213.8 5.9 %reshape.441 = f32[2,16,1,32768]{3,0,2,1:T(2,128)} reshape(f32[2,4,4,32,8,128]{5,4,3,0,2,1:T(8,128)} %copy.93) | data formatting | bytes 8388608 | tf_op jit(solution)/shard_map/reshape | solution.py:141
  219.7 19.7 %all-to-all-start.1 = ((f32[2,16,1,32768]{3,0,2,1:T(2,128)}), f32[2,16,1,32768]{3,0,2,1:T(2,128)}, u32[]{:S(2)}, u32[]{:S(2)}) async-start(f32[2,16,1,32768]{3,0,2,1:T(2,128)} %reshape.441), calls=%async_computation.1 | async-start | bytes 8388608 | tf_op jit(solution)/shard_map/all_to_all | solution.py:143
  239.4 18.3 %copy.69 = f32[4,2,128,8,512]{2,0,3,4,1:T(4,128)} copy(f32[4,2,128,8,512]{4,3,2,1,0:T(8,128)} %param.10) | data formatting | bytes 33554432 | tf_op args[2]
  257.7 17.5 %multiply_add_fusion = f32[4,2,128,8,512]{4,3,2,1,0:T(8,128)} fusion(f32[4,2,128,8,512]{4,3,2,1,0:T(8,128)} %param.9, f32[4,2,128,8,512]{4,3,2,1,0:T(8,128)} %param.10), kind=kLoop, calls=%fused_computation.6 | loop fusion | flops 8388608 | bytes 50331648 | tf_op jit(solution)/shard_map/add | solution.py:157
  275.2 41.7 %all-to-all-done.1 = f32[2,16,1,32768]{3,0,2,1:T(2,128)} async-done(((f32[2,16,1,32768]{3,0,2,1:T(2,128)}), f32[2,16,1,32768]{3,0,2,1:T(2,128)}, u32[]{:S(2)}, u32[]{:S(2)}) %all-to-all-start.1) | async-done | bytes 4194336 | tf_op jit(solution)/shard_map/all_to_all | solution.py:143
  317.0 6.6 %reshape.442 = f32[2,16,32,8,128]{4,3,2,0,1:T(8,128)} reshape(f32[2,16,1,32768]{3,0,2,1:T(2,128)} %all-to-all-done.1) | data formatting | bytes 8388608 | tf_op jit(solution)/shard_map/reshape | solution.py:145
  323.6 26.4 %fusion.14 = f32[2,128,8,512]{3,1,2,0:T(8,128)S(1)} fusion(f32[2,128,8,512]{3,2,1,0:T(8,128)} %param.8, f32[2,128,8,512]{3,1,2,0:T(8,128)} %copy-done.6, f32[2,16,32,8,128]{4,3,2,0,1:T(8,128)} %reshape.442, s32[16,32]{1,0:T(8,128)S(1)} %multiply_add_fusion.3), kind=kOutput, calls=%fused_computation.18 | convolution fusion | flops 6453985280 | bytes 16779264 | tf_op jit(solution)/shard_map/sqxdc,qxk->scdk/dot_general | solution.py:146
  354.4 11.0 %copy.68 = f32[1,2,128,8,512]{2,0,3,4,1:T(1,128)} copy(f32[1,2,128,8,512]{4,2,3,1,0:T(8,128)} %bitcast.155) | data formatting | bytes 8388608 | tf_op jit(solution)/shard_map/broadcast_in_dim | solution.py:148
  365.4 76.1 %fusion.132 = f32[5,5]{0,1:T(8,128)S(1)} fusion(f32[4,2,128,8,512]{2,0,3,4,1:T(4,128)} %copy.69, f32[1,2,128,8,512]{2,0,3,4,1:T(1,128)} %copy.68), kind=kOutput, calls=%fused_computation.158 | convolution fusion | flops 319815680 | bytes 20971620 | tf_op jit(solution)/shard_map/isyzx,jsyzx->ij/dot_general | solution.py:149
  441.5 47.8 %psum.7 = f32[5,5]{0,1:T(8,128)S(1)} all-reduce(f32[5,5]{0,1:T(8,128)S(1)} %fusion.132), channel_id=1, replica_groups=mesh['groups'=2,'gy'=4,'gz'=4] {'gy','gz'}, use_global_device_ids=true, to_apply=%region_0.2 | all-reduce | flops 25 | bytes 200 | tf_op jit(solution)/shard_map/psum | solution.py:150
  492.8 46.8 %fusion.4 = f32[1,2,128,8,512]{4,0,3,2,1:T(1,128)S(1)} fusion(f32[4,2,128,8,512]{4,3,2,1,0:T(8,128)} %multiply_add_fusion, f32[5]{0:T(128)S(1)} %broadcast_divide_fusion), kind=kOutput, calls=%fused_computation.4 | convolution fusion | flops 50331648 | bytes 20971540 | tf_op jit(solution)/shard_map/i,isyzx->syzx/dot_general | solution.py:156
  539.6 5.1 bitcast_add_fusion
  (62 shorter events, 34.0 us)
Async XLA Ops:
  2.7 6.7 %collective-permute-start = (f32[5,1,1,128]{3,2,1,0:T(1,128)S(1)}, f32[5,1,1,128]{3,2,1,0:T(1,128)S(1)}, u32[]{:S(2)}, u32[]{:S(2)}) collective-permute-start(f32[5,1,1,128]{3,2,1,0:T(1,128)S(1)} %pad_maximum_fusion.5), channel_id=1, source_target_pairs={{0,4},{4,8},{8,12},{12,0},{1,5},{5,9},{9,13},{13,1},{2,6},{6,10},{... | collective-permute-start | bytes 7688 | tf_op jit(solution)/shard_map/ppermute | solution.py:21
  5.7 3.6 collective-permute-start.1
  9.3 3.1 collective-permute-start.2
  9.4 3.1 collective-permute-start.3
  13.1 18.8 %copy-start.2 = (f32[2,128,8,512]{3,2,1,0:T(8,128)S(1)}, f32[2,128,8,512]{3,2,1,0:T(8,128)}, u32[]{:S(2)}) copy-start(f32[2,128,8,512]{3,2,1,0:T(8,128)} %param.8) | copy-start | bytes 12582916
  31.9 14.1 %copy-start.6 = (f32[2,128,8,512]{3,1,2,0:T(8,128)}, f32[2,128,8,512]{3,1,2,0:T(8,128)S(1)}, u32[]{:S(2)}) copy-start(f32[2,128,8,512]{3,1,2,0:T(8,128)S(1)} %fusion.6) | copy-start | bytes 12582916
  57.7 6.8 %copy-start.5 = (f32[4]{0:T(128)S(1)}, f32[4]{0:T(128)}, u32[]{:S(2)}) copy-start(f32[4]{0:T(128)} %param.14) | copy-start | bytes 52
  57.8 12.5 %copy-start.4 = (f32[3,4]{1,0:T(4,128)S(1)}, f32[3,4]{1,0:T(4,128)}, u32[]{:S(2)}) copy-start(f32[3,4]{1,0:T(4,128)} %param.13) | copy-start | bytes 148
  57.8 84.3 %all-to-all-start = ((f32[2,16,1,32768]{3,0,2,1:T(2,128)}), f32[2,16,1,32768]{3,0,2,1:T(2,128)}, u32[]{:S(2)}, u32[]{:S(2)}) async-start(f32[2,16,1,32768]{3,0,2,1:T(2,128)} %reshape.439), calls=%async_computation | async-start | bytes 8388608 | tf_op jit(solution)/shard_map/all_to_all | solution.py:125
  219.7 97.2 %all-to-all-start.1 = ((f32[2,16,1,32768]{3,0,2,1:T(2,128)}), f32[2,16,1,32768]{3,0,2,1:T(2,128)}, u32[]{:S(2)}, u32[]{:S(2)}) async-start(f32[2,16,1,32768]{3,0,2,1:T(2,128)} %reshape.441), calls=%async_computation.1 | async-start | bytes 8388608 | tf_op jit(solution)/shard_map/all_to_all | solution.py:143
  350.0 4.5 copy-start
  492.8 46.8 %copy-start.1 = (f32[2,128,8,512]{3,1,2,0:T(8,128)S(1)}, f32[2,128,8,512]{3,1,2,0:T(8,128)}, u32[]{:S(2)}) copy-start(f32[2,128,8,512]{3,1,2,0:T(8,128)} %copy-done) | copy-start | bytes 12582916
  492.8 46.8 %copy-start.3 = (f32[2,128,8,512]{3,2,1,0:T(8,128)S(1)}, f32[2,128,8,512]{3,2,1,0:T(8,128)}, u32[]{:S(2)}) copy-start(f32[2,128,8,512]{3,2,1,0:T(8,128)} %param.8) | copy-start | bytes 12582916
where the time goes:
time: 558 us; the launch traced here: 549 us
  matrix products  219 us (39%)
  waiting for transfers between devices  116 us (21%)
  local copies, waits for them, and re-layouts  77.4 us (14%)
  other arithmetic  49.8 us (9%)
  blocking collectives  47.8 us (9%)
  starting transfers between devices  33.4 us (6%)
  between operations  6.84 us (1%)
    dot_general x1, matrix products, body(): jnp.einsum('isyzx,jsyzx->ij', stacked, stacked, precision=PRECISE)  76.1 us
    all_to_all x1, waiting for transfers between devices, body(): lax.all_to_all(outgoing, ('gy', 'gz'), split_axis=1, concat_axis=2, tiled...  71 us
    psum x1, blocking collectives, body(): gram_matrix = lax.psum(gram_matrix, ('gy', 'gz'))  47.8 us
    dot_general x1, matrix products, body(): jnp.einsum('i,isyzx->syzx', mixing[1:], past_indirect + MIX_STEP * past_r...  46.8 us
    all_to_all x1, waiting for transfers between devices, body(): lax.all_to_all(returning, ('gy', 'gz'), split_axis=1, concat_axis=2, tile...  41.7 us
    unnamed x17, local copies, waits for them, and re-layouts  27.2 us
    dot_general x1, matrix products, body(): jnp.einsum('sqxdc,qxk->scdk', pieces, table_back, precision=PRECISE)  26.4 us
    another operation x2, other arithmetic, couple(): jnp.stack([oxygen * spectrum[0] + mixed_site * spectrum[1], mixed_site *...  23.2 us
  transfers between devices with their start and end apart: 6, of which 4 were waited for; matrix products, arithmetic and copies ran while one was open for 7% of the time, Pallas kernels for 0%

commit v1 on v0

--- a/solution.py
+++ b/solution.py
@@ -122,7 +122,12 @@
         "scdx,xqk->sqkdc", direct, table_x.reshape(cells_x, blocks, width_x), precision=PRECISE
     )
     outgoing = outgoing.reshape(2, blocks, 1, width_x * cells_z * cells_y)
-    received = lax.all_to_all(outgoing, ("gy", "gz"), split_axis=1, concat_axis=2, tiled=True)
+    received = jnp.concatenate(
+        lax.all_to_all(
+            jnp.stack(jnp.split(outgoing, lax.axis_size(("gy", "gz")), axis=1)), ("gy", "gz"), 0, 0
+        ),
+        axis=2,
+    )
     count = received.shape[0]
     pieces = received.reshape(count, parts_y, parts_z, width_x, cells_z, cells_y)
     partial_value = jnp.einsum("sabxdc,acy->sbxdy", pieces, grid_y, precision=PRECISE)

time: 558 us -> 578 us (1.036)
  local copies, waits for them, and re-layouts: 77.4 us -> 97 us
    unnamed x17 -> x34, local copies, waits for them, and re-layouts: 27.2 us -> 53.8 us
    reshape x1 -> x0, local copies, waits for them, and re-layouts: 7.04 us -> none  [body(): received.reshape(count, parts_y, parts_z, width_x, cells_z, cells_y)]
    reshape x2 -> x1, local copies, waits for them, and re-layouts: 11.7 us -> 4.94 us  [body(): outgoing = outgoing.reshape(2, blocks, 1, width_x * cells_z * cells_y)]
    transpose x0 -> x1, local copies, waits for them, and re-layouts: none -> 5.81 us  [body(): jnp.einsum('scdx,xqk->sqkdc', direct, table_x.reshape(cells_x, blocks, wi...]
where the time goes in v1:
time: 578 us; the launch traced here: 570 us
  matrix products  219 us (38%)
  waiting for transfers between devices  115 us (20%)
  local copies, waits for them, and re-layouts  97 us (17%)
  other arithmetic  50.4 us (9%)
  blocking collectives  47.7 us (8%)
  starting transfers between devices  33.8 us (6%)
  between operations  7.04 us (1%)
    dot_general x1, matrix products, body(): jnp.einsum('isyzx,jsyzx->ij', stacked, stacked, precision=PRECISE)  76.1 us
    all_to_all x1, waiting for transfers between devices, body(): lax.all_to_all(jnp.stack(jnp.split(outgoing, lax.axis_size(('gy', 'gz')),...  70.3 us
    unnamed x34, local copies, waits for them, and re-layouts  53.8 us
    psum x1, blocking collectives, body(): gram_matrix = lax.psum(gram_matrix, ('gy', 'gz'))  47.7 us
    dot_general x1, matrix products, body(): jnp.einsum('i,isyzx->syzx', mixing[1:], past_indirect + MIX_STEP * past_r...  46.8 us
    all_to_all x1, waiting for transfers between devices, body(): lax.all_to_all(returning, ('gy', 'gz'), split_axis=1, concat_axis=2, tile...  41.7 us
    dot_general x1, matrix products, body(): jnp.einsum('sqxdc,qxk->scdk', pieces, table_back, precision=PRECISE)  26.4 us
    another operation x2, other arithmetic, couple(): jnp.stack([oxygen * spectrum[0] + mixed_site * spectrum[1], mixed_site *...  23.6 us
  transfers between devices with their start and end apart: 6, of which 4 were waited for; matrix products, arithmetic and copies ran while one was open for 7% of the time, Pallas kernels for 0%

profile of v1, /device:TPU:0, one launch (start us, length us, event | category | flops | bytes accessed | tf_op | source)
XLA Modules:
  0.0 569.6 jit_solution(10481851244231089377)
XLA Ops:
  13.1 18.8 %fusion.6 = f32[2,128,8,512]{3,1,2,0:T(8,128)S(1)} fusion(f32[8,1152]{1,0:T(8,128)S(1)} %fusion.240, f32[2,128,1152]{2,1,0:T(8,128)S(1)} %broadcast_multiply_fusion, f32[1152]{0:T(1024)S(1)} %sub.111, f32[512]{0:T(512)S(1)} %iota_convert_fusion), kind=kOutput, calls=%fused_computation.8 | convolution fusion | flops 14503182336 | bytes 5417472 | tf_op jit(solution)/shard_map/sra,xa->srx/dot_general | solution.py:83
  31.9 14.1 %fusion.56 = f32[2,16,32,8,128]{4,2,3,0,1:T(8,128)S(1)} fusion(f32[2,128,8,512]{3,1,2,0:T(8,128)S(1)} %fusion.6, f32[2,128,8,512]{3,2,1,0:T(8,128)S(1)} %copy-done.3, s32[16,32]{1,0:T(8,128)S(1)} %multiply_add_fusion.3), kind=kOutput, calls=%fused_computation.68 | convolution fusion | flops 6451888128 | bytes 12584960 | tf_op jit(solution)/shard_map/scdx,xqk->sqkdc/dot_general | solution.py:121
  46.0 5.8 %copy.87 = f32[2,16,32,8,128]{4,3,2,1,0:T(8,128)} copy(f32[2,16,32,8,128]{4,2,3,0,1:T(8,128)S(1)} %fusion.56) | data formatting | bytes 8388608 | tf_op jit(solution)/shard_map/scdx,xqk->sqkdc/transpose | solution.py:121
  51.8 4.9 reshape.412
  84.3 7.2 %all-to-all-start = ((f32[16,2,1,1,32768]{4,2,3,1,0:T(1,128)}), f32[16,2,1,1,32768]{4,2,3,1,0:T(1,128)}, u32[]{:S(2)}, u32[]{:S(2)}) async-start(f32[16,2,1,1,32768]{4,2,3,1,0:T(1,128)} %fusion.220), calls=%async_computation | async-start | bytes 8388608 | tf_op jit(solution)/shard_map/all_to_all | solution.py:126
  98.3 70.3 %all-to-all-done = f32[16,2,1,1,32768]{4,2,3,1,0:T(1,128)} async-done(((f32[16,2,1,1,32768]{4,2,3,1,0:T(1,128)}), f32[16,2,1,1,32768]{4,2,3,1,0:T(1,128)}, u32[]{:S(2)}, u32[]{:S(2)}) %all-to-all-start) | async-done | bytes 4194336 | tf_op jit(solution)/shard_map/all_to_all | solution.py:126
  168.6 13.7 %fusion.23 = f32[2,4,32,8,512,1]{4,3,5,1,2,0:T(8,128)S(1)} fusion(f32[2,4,4,32,8,128]{5,4,3,0,2,1:T(8,128)} %bitcast.55, s32[4,128]{1,0:T(4,128)S(1)} %multiply_add_fusion.5), kind=kOutput, calls=%fused_computation.28 | convolution fusion | flops 6446645248 | bytes 8390656 | tf_op jit(solution)/shard_map/sabxdc,acy->sbxdy/dot_general | solution.py:133
  186.7 10.6 %fusion.90 = f32[1,32,32,512]{3,2,1,0:T(8,128)S(1)} fusion(f32[2,32,32,512]{3,2,1,0:T(8,128)S(1)} %fusion.59, f32[]{:T(128)} %bitcast.14, f32[]{:T(128)} %bitcast.13, f32[]{:T(128)} %bitcast.12, f32[]{:T(128)} %bitcast.11, f32[]{:T(128)} %bitcast.10, f32[]{:T(128)} %bitcast.9, f32[]{:T(128)} %bitcast.8, f32[512]{0:T(512)S(1)} %fusion.256, ...), kind=kLoop, calls=%fused_computation.96 | loop fusion | flops 31457280 | bytes 6297648 | tf_op jit(solution)/shard_map/stack | solution.py:59
  197.3 13.0 %fusion.101 = f32[1,32,32,512]{3,2,1,0:T(8,128)S(1)} fusion(f32[2,32,32,512]{3,2,1,0:T(8,128)S(1)} %fusion.59, f32[]{:T(128)} %bitcast.74, f32[]{:T(128)} %bitcast.73, f32[]{:T(128)} %bitcast.72, f32[]{:T(128)} %bitcast.71, f32[]{:T(128)} %bitcast.14, f32[]{:T(128)} %bitcast.12, f32[]{:T(128)} %bitcast.10, f32[]{:T(128)} %bitcast.8, f32[512]{0:T(512)S(1)} %fusion.256, ...), kind=kLoop, calls=%fused_computation.107 | loop fusion | flops 50331648 | bytes 6297648 | tf_op jit(solution)/shard_map/stack | solution.py:59
  214.4 13.6 %fusion.63 = f32[2,4,4,32,8,128]{5,3,4,2,0,1:T(8,128)S(1)} fusion(f32[2,32,4,8,512]{4,3,1,0,2:T(8,128)S(1)} %fusion.62, s32[4,128]{1,0:T(4,128)S(1)} %multiply_add_fusion.5), kind=kOutput, calls=%fused_computation.71 | convolution fusion | flops 6446645248 | bytes 8390656 | tf_op jit(solution)/shard_map/sxbdy,acy->sabxdc/dot_general | solution.py:145
  227.9 5.8 %copy.138 = f32[2,4,4,32,8,128]{5,4,3,0,2,1:T(8,128)} copy(f32[2,4,4,32,8,128]{5,3,4,2,0,1:T(8,128)S(1)} %fusion.63) | data formatting | bytes 8388608 | tf_op jit(solution)/shard_map/reshape | solution.py:146
  233.8 5.9 %reshape.435 = f32[2,16,1,32768]{3,0,2,1:T(2,128)} reshape(f32[2,4,4,32,8,128]{5,4,3,0,2,1:T(8,128)} %copy.138) | data formatting | bytes 8388608 | tf_op jit(solution)/shard_map/reshape | solution.py:146
  239.7 19.7 %all-to-all-start.1 = ((f32[2,16,1,32768]{3,0,2,1:T(2,128)}), f32[2,16,1,32768]{3,0,2,1:T(2,128)}, u32[]{:S(2)}, u32[]{:S(2)}) async-start(f32[2,16,1,32768]{3,0,2,1:T(2,128)} %reshape.435), calls=%async_computation.1 | async-start | bytes 8388608 | tf_op jit(solution)/shard_map/all_to_all | solution.py:148
  259.4 18.3 %copy.114 = f32[4,2,128,8,512]{2,0,3,4,1:T(4,128)} copy(f32[4,2,128,8,512]{4,3,2,1,0:T(8,128)} %param.10) | data formatting | bytes 33554432 | tf_op args[2]
  277.7 17.5 %multiply_add_fusion = f32[4,2,128,8,512]{4,3,2,1,0:T(8,128)} fusion(f32[4,2,128,8,512]{4,3,2,1,0:T(8,128)} %param.9, f32[4,2,128,8,512]{4,3,2,1,0:T(8,128)} %param.10), kind=kLoop, calls=%fused_computation.6 | loop fusion | flops 8388608 | bytes 50331648 | tf_op jit(solution)/shard_map/add | solution.py:162
  295.2 41.7 %all-to-all-done.1 = f32[2,16,1,32768]{3,0,2,1:T(2,128)} async-done(((f32[2,16,1,32768]{3,0,2,1:T(2,128)}), f32[2,16,1,32768]{3,0,2,1:T(2,128)}, u32[]{:S(2)}, u32[]{:S(2)}) %all-to-all-start.1) | async-done | bytes 4194336 | tf_op jit(solution)/shard_map/all_to_all | solution.py:148
  336.9 6.6 %reshape.436 = f32[2,16,32,8,128]{4,3,2,0,1:T(8,128)} reshape(f32[2,16,1,32768]{3,0,2,1:T(2,128)} %all-to-all-done.1) | data formatting | bytes 8388608 | tf_op jit(solution)/shard_map/reshape | solution.py:150
  343.5 26.4 %fusion.14 = f32[2,128,8,512]{3,1,2,0:T(8,128)S(1)} fusion(f32[2,128,8,512]{3,2,1,0:T(8,128)} %param.8, f32[2,128,8,512]{3,1,2,0:T(8,128)} %copy-done.7, f32[2,16,32,8,128]{4,3,2,0,1:T(8,128)} %reshape.436, s32[16,32]{1,0:T(8,128)S(1)} %multiply_add_fusion.3), kind=kOutput, calls=%fused_computation.18 | convolution fusion | flops 6453985280 | bytes 16779264 | tf_op jit(solution)/shard_map/sqxdc,qxk->scdk/dot_general | solution.py:151
  369.9 4.4 copy.120
  374.4 11.0 %copy.113 = f32[1,2,128,8,512]{2,0,3,4,1:T(1,128)} copy(f32[1,2,128,8,512]{4,2,3,1,0:T(8,128)} %bitcast.232) | data formatting | bytes 8388608 | tf_op jit(solution)/shard_map/broadcast_in_dim | solution.py:153
  385.4 76.1 %fusion.132 = f32[5,5]{0,1:T(8,128)S(1)} fusion(f32[4,2,128,8,512]{2,0,3,4,1:T(4,128)} %copy.114, f32[1,2,128,8,512]{2,0,3,4,1:T(1,128)} %copy.113), kind=kOutput, calls=%fused_computation.158 | convolution fusion | flops 319815680 | bytes 20971620 | tf_op jit(solution)/shard_map/isyzx,jsyzx->ij/dot_general | solution.py:154
  461.4 47.7 %psum.7 = f32[5,5]{0,1:T(8,128)S(1)} all-reduce(f32[5,5]{0,1:T(8,128)S(1)} %fusion.132), channel_id=1, replica_groups=mesh['groups'=2,'gy'=4,'gz'=4] {'gy','gz'}, use_global_device_ids=true, to_apply=%region_0.2 | all-reduce | flops 25 | bytes 200 | tf_op jit(solution)/shard_map/psum | solution.py:155
  513.0 46.8 %fusion.4 = f32[1,2,128,8,512]{4,0,3,2,1:T(1,128)S(1)} fusion(f32[4,2,128,8,512]{4,3,2,1,0:T(8,128)} %multiply_add_fusion, f32[5]{0:T(128)S(1)} %broadcast_divide_fusion), kind=kOutput, calls=%fused_computation.4 | convolution fusion | flops 50331648 | bytes 20971540 | tf_op jit(solution)/shard_map/i,isyzx->syzx/dot_general | solution.py:161
  559.8 5.1 bitcast_add_fusion
  (79 shorter events, 57.4 us)
Async XLA Ops:
  2.7 6.7 %collective-permute-start = (f32[5,1,1,128]{3,2,1,0:T(1,128)S(1)}, f32[5,1,1,128]{3,2,1,0:T(1,128)S(1)}, u32[]{:S(2)}, u32[]{:S(2)}) collective-permute-start(f32[5,1,1,128]{3,2,1,0:T(1,128)S(1)} %pad_maximum_fusion.5), channel_id=1, source_target_pairs={{0,4},{4,8},{8,12},{12,0},{1,5},{5,9},{9,13},{13,1},{2,6},{6,10},{... | collective-permute-start | bytes 7688 | tf_op jit(solution)/shard_map/ppermute | solution.py:21
  5.7 3.6 collective-permute-start.1
  9.3 3.1 collective-permute-start.2
  9.4 3.1 collective-permute-start.3
  13.1 18.8 %copy-start.3 = (f32[2,128,8,512]{3,2,1,0:T(8,128)S(1)}, f32[2,128,8,512]{3,2,1,0:T(8,128)}, u32[]{:S(2)}) copy-start(f32[2,128,8,512]{3,2,1,0:T(8,128)} %param.8) | copy-start | bytes 12582916
  31.9 14.1 %copy-start.7 = (f32[2,128,8,512]{3,1,2,0:T(8,128)}, f32[2,128,8,512]{3,1,2,0:T(8,128)S(1)}, u32[]{:S(2)}) copy-start(f32[2,128,8,512]{3,1,2,0:T(8,128)S(1)} %fusion.6) | copy-start | bytes 12582916
  56.8 20.2 %copy-start.2 = (f32[2,16,1,32768]{3,1,0,2:T(8,128)S(1)}, f32[2,16,1,32768]{3,1,0,2:T(8,128)}, u32[]{:S(2)}) copy-start(f32[2,16,1,32768]{3,1,0,2:T(8,128)} %reshape.412) | copy-start | bytes 12582916
  84.3 7.2 %copy-start.6 = (f32[4]{0:T(128)S(1)}, f32[4]{0:T(128)}, u32[]{:S(2)}) copy-start(f32[4]{0:T(128)} %param.14) | copy-start | bytes 52
  84.3 13.2 %copy-start.5 = (f32[3,4]{1,0:T(4,128)S(1)}, f32[3,4]{1,0:T(4,128)}, u32[]{:S(2)}) copy-start(f32[3,4]{1,0:T(4,128)} %param.13) | copy-start | bytes 148
  84.3 84.3 %all-to-all-start = ((f32[16,2,1,1,32768]{4,2,3,1,0:T(1,128)}), f32[16,2,1,1,32768]{4,2,3,1,0:T(1,128)}, u32[]{:S(2)}, u32[]{:S(2)}) async-start(f32[16,2,1,1,32768]{4,2,3,1,0:T(1,128)} %fusion.220), calls=%async_computation | async-start | bytes 8388608 | tf_op jit(solution)/shard_map/all_to_all | solution.py:126
  239.7 97.2 %all-to-all-start.1 = ((f32[2,16,1,32768]{3,0,2,1:T(2,128)}), f32[2,16,1,32768]{3,0,2,1:T(2,128)}, u32[]{:S(2)}, u32[]{:S(2)}) async-start(f32[2,16,1,32768]{3,0,2,1:T(2,128)} %reshape.435), calls=%async_computation.1 | async-start | bytes 8388608 | tf_op jit(solution)/shard_map/all_to_all | solution.py:148
  369.9 4.5 copy-start
  513.0 46.8 %copy-start.1 = (f32[2,128,8,512]{3,1,2,0:T(8,128)S(1)}, f32[2,128,8,512]{3,1,2,0:T(8,128)}, u32[]{:S(2)}) copy-start(f32[2,128,8,512]{3,1,2,0:T(8,128)} %copy-done) | copy-start | bytes 12582916
  513.0 46.8 %copy-start.4 = (f32[2,128,8,512]{3,2,1,0:T(8,128)S(1)}, f32[2,128,8,512]{3,2,1,0:T(8,128)}, u32[]{:S(2)}) copy-start(f32[2,128,8,512]{3,2,1,0:T(8,128)} %param.8) | copy-start | bytes 12582916
